TPU v7x, 32 devices: a whole 2x2x4 slice. The times are simulated.
32 devices in a mesh: grp: 2 (over y), pos: 16 (over z, x, core).
Axes of the slice: x: 2, y: 2, z: 4, core: 2. Of those that a mesh axis runs over, the one named last changes fastest.
Arguments:
- object_field: float32 [2, 2048, 2048], P(None, 'grp', 'pos'), may hold values from -5 to 5
- probe_field: float32 [2, 256, 256], replicated, may hold values from -5 to 5
- patterns: float32 [96, 256, 256], P(('grp', 'pos')), may hold values from 0.05 to 5
- corners: int32 [2, 96], P(None, ('grp', 'pos')), may hold values from 0 to 1792, as said below
- counts: int32 [32], replicated, may hold values from 1 to 3, as said below
Outputs:
- object_new: float32 [2, 2048, 2048], P(None, 'grp', 'pos')
- probe_new: float32 [2, 256, 256], replicated
Inputs may be any that keep to these rules, and one draw needn't show every extreme that they name: `corners`: each slot's patch of 256 x 256 cells lies inside the object and inside its device's block of 1024 x 128 object cells extended by 128 cells on every side (the device at grp index a and pos index b holds rows a * 1024 to a * 1024 + 1023 and columns b * 128 to b * 128 + 127). The live slots of a device are its first counts[d] slots; some device has all 3 slots live.
All inputs are finite; a program needn't handle non-finite values.
Results may differ from a plain program's by a relative error of at most 0.00012.
Values sent between devices are 32-bit elements; how exact they have to be, the bound alone decides.
A program may use at most 64 MiB of HBM per device.

v0:
```python
import math
import jax
import jax.numpy as jnp
from jax import lax
from jax.sharding import PartitionSpec as P

M = 256
HALO = 128
step_object = 0.25
step_probe = 4.0


def padded(x, sides, width):
    for axis, dim in sides:
        peers, length = (lax.axis_size(axis), x.shape[dim])
        up = [(i, (i + 1) % peers) for i in range(peers - 1)]
        down = [(j, i) for i, j in up]
        last = lax.slice_in_dim(x, length - width, length, axis=dim)
        initial = lax.slice_in_dim(x, 0, width, axis=dim)
        before = lax.ppermute(last, axis, up)
        after = lax.ppermute(initial, axis, down)
        x = jnp.concatenate([before, x, after], axis=dim)
    return x


def product(left, right):
    return jnp.dot(left, right, precision=lax.Precision.HIGHEST, preferred_element_type=jnp.float32)


def left_mul(cos_part, sin_part, real_part, imag_part):
    return (
        product(cos_part, real_part) - product(sin_part, imag_part),
        product(cos_part, imag_part) + product(sin_part, real_part),
    )


def right_mul(real_part, imag_part, cos_part, sin_part):
    return (
        product(real_part, cos_part) - product(imag_part, sin_part),
        product(real_part, sin_part) + product(imag_part, cos_part),
    )


def dft_tables(order):
    indices = jnp.arange(order, dtype=jnp.int32)
    phases = indices[:, None] * indices[None, :] % order
    angles = phases.astype(jnp.float32) * (2.0 * math.pi / order)
    factor = 1.0 / math.sqrt(order)
    return (jnp.cos(angles) * factor, -jnp.sin(angles) * factor)


def far_field(wave, measured, cos_table, sin_table):
    front_re, front_im = left_mul(cos_table, sin_table, wave[0], wave[1])
    far_re, far_im = right_mul(front_re, front_im, cos_table, sin_table)
    excess = far_re * far_re + far_im * far_im - measured
    back_re, back_im = left_mul(cos_table, -sin_table, excess * far_re, excess * far_im)
    chi_re, chi_im = right_mul(back_re, back_im, cos_table, -sin_table)
    return jnp.stack((chi_re, chi_im))


def on_device(object_field, probe_field, patterns, corners, counts):
    tile_rows = object_field.shape[1]
    tile_cols = object_field.shape[2]
    slot_count = patterns.shape[0]
    pos_count = lax.axis_size("pos")
    grp_index = lax.axis_index("grp")
    pos_index = lax.axis_index("pos")
    device = grp_index * pos_count + pos_index
    own_count = counts[device]
    cos_table, sin_table = dft_tables(M)
    extended = padded(object_field, (("grp", 1), ("pos", 2)), HALO)
    row_local = corners[0] - grp_index * tile_rows + HALO
    col_local = corners[1] - pos_index * tile_cols + HALO

    def cut_patch(row_at, col_at):
        return lax.dynamic_slice(extended, (jnp.int32(0), row_at, col_at), (2, M, M))

    patches = jax.vmap(cut_patch)(row_local, col_local)
    waves = jnp.stack(
        (
            probe_field[0] * patches[:, 0] - probe_field[1] * patches[:, 1],
            probe_field[0] * patches[:, 1] + probe_field[1] * patches[:, 0],
        ),
        axis=1,
    )
    empty_results = jnp.zeros((slot_count, 2, M, M), jnp.float32)

    def solve_own(step, results):
        result = far_field(waves[step], patterns[step], cos_table, sin_table)
        return lax.dynamic_update_index_in_dim(results, result, step, 0)

    residuals = lax.fori_loop(0, own_count, solve_own, empty_results)

    def accumulate(step, totals):
        grad_ext, grad_probe = totals
        chi_re = residuals[step, 0]
        chi_im = residuals[step, 1]
        patch_re = patches[step, 0]
        patch_im = patches[step, 1]
        obj_part = jnp.stack(
            (
                probe_field[0] * chi_re + probe_field[1] * chi_im,
                probe_field[0] * chi_im - probe_field[1] * chi_re,
            )
        )
        prb_part = jnp.stack(
            (patch_re * chi_re + patch_im * chi_im, patch_re * chi_im - patch_im * chi_re)
        )
        anchor = (jnp.int32(0), row_local[step], col_local[step])
        current = lax.dynamic_slice(grad_ext, anchor, (2, M, M))
        grad_ext = lax.dynamic_update_slice(grad_ext, current + obj_part, anchor)
        return (grad_ext, grad_probe + prb_part)

    start_totals = (
        jnp.zeros(extended.shape, jnp.float32),
        jnp.zeros(probe_field.shape, jnp.float32),
    )
    grad_ext, grad_probe = lax.fori_loop(0, own_count, accumulate, start_totals)
    col_rims = jnp.concatenate((grad_ext[:, :, :HALO], grad_ext[:, :, -HALO:]), axis=2)
    col_arrived = padded(col_rims, (("pos", 2),), HALO)
    middle = grad_ext[:, :, HALO : HALO + tile_cols]
    middle = middle.at[:, :, :HALO].add(col_arrived[:, :, :HALO])
    middle = middle.at[:, :, tile_cols - HALO :].add(col_arrived[:, :, -HALO:])
    row_rims = jnp.concatenate((middle[:, :HALO], middle[:, -HALO:]), axis=1)
    row_arrived = padded(row_rims, (("grp", 1),), HALO)
    core = middle[:, HALO : HALO + tile_rows]
    core = core.at[:, :HALO].add(row_arrived[:, :HALO])
    core = core.at[:, tile_rows - HALO :].add(row_arrived[:, -HALO:])
    object_new = object_field - step_object * core
    live_total = jnp.sum(counts).astype(jnp.float32)
    share = lax.psum_scatter(grad_probe, "pos", scatter_dimension=1, tiled=True)
    share = lax.psum(share, "grp")
    row_share = M // pos_count
    mine = lax.dynamic_slice_in_dim(probe_field, pos_index * row_share, row_share, 1)
    new_rows = mine - step_probe * share / live_total
    probe_new = lax.all_gather(new_rows, "pos", axis=1, tiled=True)
    return (object_new, probe_new)


def solution(mesh):
    return jax.shard_map(
        on_device,
        mesh=mesh,
        in_specs=(
            P(None, "grp", "pos"),
            P(),
            P(("grp", "pos"), None, None),
            P(None, ("grp", "pos")),
            P(),
        ),
        out_specs=(P(None, "grp", "pos"), P()),
        check_vma=False,
    )
```

profile of v0, /device:TPU:0, one launch (start us, length us, event | category | flops | bytes accessed | tf_op | source)
XLA Modules:
  0.0 322.7 jit_solution(2919764576730867751)
XLA Ops:
  8.3 4.9 %collective-permute-start = (f32[2,128,128]{2,1,0:T(8,128)S(1)}, f32[2,128,128]{2,1,0:T(8,128)S(1)}, u32[]{:S(2)}, u32[]{:S(2)}) collective-permute-start(f32[2,128,128]{2,1,0:T(8,128)S(1)} %get-tuple-element.348), channel_id=1, source_target_pairs={{0,16},{1,17},{2,18},{3,19},{4,20},{5,21},{6,22},{7,23},{8,24},{9,... | collective-permute-start | bytes 393224 | tf_op jit(solution)/shard_map/ppermute | solution.py:20
  17.2 2.8 collective-permute-done.1
  24.4 3.7 %collective-permute-done.3 = f32[2,1280,128]{2,1,0:T(8,128)} collective-permute-done((f32[2,1280,128]{2,1,0:T(8,128)S(1)}, f32[2,1280,128]{2,1,0:T(8,128)}, u32[]{:S(2)}, u32[]{:S(2)}) %collective-permute-start.3) | collective-permute-done | bytes 1310752 | tf_op jit(solution)/shard_map/ppermute | solution.py:21
  28.2 3.4 %pad_maximum_fusion = f32[2,1280,384]{2,1,0:T(8,128)} fusion(f32[2,1280,128]{2,1,0:T(8,128)} %collective-permute-done.3, f32[2,1280,128]{2,1,0:T(8,128)S(1)} %constant_dynamic-update-slice_fusion, f32[2,1280,128]{2,1,0:T(8,128)S(1)} %collective-permute-done.2), kind=kLoop, calls=%fused_computation.139 | loop fusion | flops 1966080 | bytes 7864320 | tf_op jit(solution)/shard_map/concatenate | solution.py:22
  31.8 9.6 %while.33 = (s32[]{:T(128)}, f32[2,1280,384]{2,1,0:T(8,128)}, s32[3,3]{1,0:T(4,128)S(1)}, f32[3,2,256,256]{3,2,1,0:T(8,128)S(1)}, s32[]{:T(128)}) while((s32[]{:T(128)}, f32[2,1280,384]{2,1,0:T(8,128)}, s32[3,3]{1,0:T(4,128)S(1)}, f32[3,2,256,256]{3,2,1,0:T(8,128)S(1)}, s32[]{:T(128)}) %tuple.101), condition=%wide.while_cond.4, body=%wide.while_body.4.sunk | while | flops 2 | bytes 1048693 | solution.py:76
  32.4 2.5 bitcast_dynamic-update-slice_fusion.2
  35.7 2.5 bitcast_dynamic-update-slice_fusion.2
  38.9 2.5 bitcast_dynamic-update-slice_fusion.2
  44.2 30.9 %while.34 = (s32[]{:T(128)}, f32[3,2,256,256]{3,2,1,0:T(8,128)}, s32[]{:T(128)}, f32[3,2,256,256]{3,2,1,0:T(8,128)}, f32[3,256,256]{2,1,0:T(8,128)}, /*index=5*/s32[]{:T(128)}, s32[]{:T(128)}, s32[]{:T(128)}, s32[]{}) while((s32[]{:T(128)}, f32[3,2,256,256]{3,2,1,0:T(8,128)}, s32[]{:T(128)}, ...), condition=%wide.region_1.2_spmd.clone.clone, body=%wide.region_0.1_spmd.clone.clone.sunk | while | flops 3238789120 | bytes 12320939 | solution.py:92
  44.9 2.4 fusion.179
  47.3 2.4 convolution_subtract_fusion.7
  51.2 2.4 fusion.181
  53.7 2.4 convolution_add_fusion.6
  56.1 1.5 convolution_subtract_fusion.8
  57.6 1.5 fusion.182
  59.1 2.4 fusion.183
  63.0 1.5 convolution_add_fusion.7
  66.0 1.5 convolution_subtract_fusion.9
  68.9 1.5 fusion.189
  70.4 1.5 fusion.185
  71.9 1.5 fusion.187
  75.1 2.1 broadcast_in_dim.18
  77.3 14.2 %while.32 = (s32[]{:T(128)}, f32[2,1280,384]{2,1,0:T(8,128)}, f32[2,256,256]{2,1,0:T(8,128)S(1)}, s32[]{:T(128)}, s32[3]{0:T(128)S(1)}, /*index=5*/s32[3]{0:T(12...) while((s32[]{:T(128)}, f32[2,1280,384]{2,1,0:T(8,128)}, ...), condition=%wide.region_3.4_spmd, body=%wide.region_2.3_spmd.sunk | while | flops 1310731 | bytes 6816019 | solution.py:118
  85.6 5.2 %dynamic_update_slice.13 = f32[2,1280,384]{2,1,0:T(8,128)} dynamic-update-slice(f32[2,1280,384]{2,1,0:T(8,128)} %get-tuple-element.545, f32[2,256,256]{2,1,0:T(8,128)S(1)} %get-tuple-element.473, s32[]{:T(128)} %constant.180.clone.1..sunk, s32[]{:T(128)S(6)} %select_n.163, s32[]{:T(128)S(6)} %select_n.164) | dynamic-update-slice | bytes 1048580 | tf_op jit(solution)/shard_map/while/body/dynamic_update_slice | solution.py:111
  91.5 3.2 fusion.116
  94.7 27.6 %collective-permute-start.4 = (f32[2,1280,128]{2,1,0:T(8,128)}, f32[2,1280,128]{2,1,0:T(8,128)S(1)}, u32[]{:S(2)}, u32[]{:S(2)}) collective-permute-start(f32[2,1280,128]{2,1,0:T(8,128)} %get-tuple-element.341), channel_id=1, source_target_pairs={{0,1},{1,2},{2,3},{3,4},{4,5},{5,6},{6,7},{7,8},{8,9},{9,10},{10,1... | collective-permute-start | bytes 3932168 | tf_op jit(solution)/shard_map/ppermute | solution.py:20
  124.9 147.0 %reduce-scatter.2.cloned.1.call-done = f32[2,16,256]{2,1,0:T(8,128)} async-done(((f32[2,256,256]{2,1,0:T(8,128)}), f32[2,16,256]{2,1,0:T(8,128)}) %reduce-scatter.2.cloned.1.call-update) | async-done | bytes 32784 | tf_op jit(solution)/shard_map/reduce_scatter | solution.py:131
  271.9 9.0 %psum.7 = f32[2,16,256]{2,1,0:T(8,128)S(1)} all-reduce(f32[2,16,256]{2,1,0:T(8,128)} %reduce-scatter.2.cloned.1.call-done), channel_id=1, replica_groups=mesh['grp'=2,'pos'=16] {'grp'}, use_global_device_ids=true, to_apply=%region_5.6 | all-reduce | flops 8192 | bytes 65536 | tf_op jit(solution)/shard_map/psum | solution.py:132
  280.9 1.9 add_add_fusion
  282.8 2.5 collective-permute-start.6
  285.3 20.9 %all_gather.3 = f32[2,256,256]{2,1,0:T(8,128)S(1)} all-gather(f32[2,16,256]{2,1,0:T(8,128)S(1)} %divide_subtract_fusion), channel_id=1, replica_groups=mesh['grp'=2,'pos'=16] {'pos'}, dimensions={1}, use_global_device_ids=true | all-gather | bytes 557056 | tf_op jit(solution)/shard_map/all_gather | solution.py:136
  307.7 6.3 %collective-permute-done.7 = f32[2,128,128]{2,1,0:T(8,128)S(1)} collective-permute-done((f32[2,128,128]{2,1,0:T(8,128)S(1)}, f32[2,128,128]{2,1,0:T(8,128)S(1)}, u32[]{:S(2)}, u32[]{:S(2)}) %collective-permute-start.7) | collective-permute-done | bytes 131104 | tf_op jit(solution)/shard_map/ppermute | solution.py:21
  (65 shorter events, 30.2 us)
Async XLA Ops:
  7.2 15.6 %copy-start.5 = (s32[2,3]{1,0:T(2,128)S(1)}, s32[2,3]{1,0:T(2,128)}, u32[]{:S(2)}) copy-start(s32[2,3]{1,0:T(2,128)} %param.24) | copy-start | bytes 76
  7.2 15.7 %copy-start.6 = (s32[32]{0:T(128)S(1)}, s32[32]{0:T(128)}, u32[]{:S(2)}) copy-start(s32[32]{0:T(128)} %param.25) | copy-start | bytes 388
  7.2 16.4 %copy-start.1 = (f32[2,256,256]{2,1,0:T(8,128)S(1)}, f32[2,256,256]{2,1,0:T(8,128)}, u32[]{:S(2)}) copy-start(f32[2,256,256]{2,1,0:T(8,128)} %param.22) | copy-start | bytes 1572868
  7.2 264.7 %reduce-scatter.2.cloned.1.call-start = ((), (), s32[]{:S(2)}) async-start(), calls=%async_computation.1 | async-start | bytes 557056 | tf_op jit(solution)/shard_map/reduce_scatter | solution.py:131
  8.3 7.6 %collective-permute-start = (f32[2,128,128]{2,1,0:T(8,128)S(1)}, f32[2,128,128]{2,1,0:T(8,128)S(1)}, u32[]{:S(2)}, u32[]{:S(2)}) collective-permute-start(f32[2,128,128]{2,1,0:T(8,128)S(1)} %get-tuple-element.348), channel_id=1, source_target_pairs={{0,16},{1,17},{2,18},{3,19},{4,20},{5,21},{6,22},{7,23},{8,24},{9,... | collective-permute-start | bytes 393224 | tf_op jit(solution)/shard_map/ppermute | solution.py:20
  13.2 6.9 %collective-permute-start.1 = (f32[2,128,128]{2,1,0:T(8,128)S(1)}, f32[2,128,128]{2,1,0:T(8,128)S(1)}, u32[]{:S(2)}, u32[]{:S(2)}) collective-permute-start(f32[2,128,128]{2,1,0:T(8,128)S(1)} %get-tuple-element.347), channel_id=1, source_target_pairs={{16,0},{17,1},{18,2},{19,3},{20,4},{21,5},{22,6},{23,7},{24,8},{25... | collective-permute-start | bytes 393224 | tf_op jit(solution)/shard_map/ppermute | solution.py:21
  20.1 4.3 %collective-permute-start.2 = (f32[2,1280,128]{2,1,0:T(8,128)S(1)}, f32[2,1280,128]{2,1,0:T(8,128)S(1)}, u32[]{:S(2)}, u32[]{:S(2)}) collective-permute-start(f32[2,1280,128]{2,1,0:T(8,128)S(1)} %constant_dynamic-update-slice_fusion), channel_id=1, source_target_pairs={{0,1},{1,2},{2,3},{3,4},{4,5},{5,6},{6,7},{7,8},{8,9},{9,10},{10,1... | collective-permute-start | bytes 3932168 | tf_op jit(solution)/shard_map/ppermute | solution.py:20
  21.5 6.7 %collective-permute-start.3 = (f32[2,1280,128]{2,1,0:T(8,128)S(1)}, f32[2,1280,128]{2,1,0:T(8,128)}, u32[]{:S(2)}, u32[]{:S(2)}) collective-permute-start(f32[2,1280,128]{2,1,0:T(8,128)S(1)} %constant_dynamic-update-slice_fusion), channel_id=1, source_target_pairs={{1,0},{2,1},{3,2},{4,3},{5,4},{6,5},{7,6},{8,7},{9,8},{10,9},{11,1... | collective-permute-start | bytes 3932168 | tf_op jit(solution)/shard_map/ppermute | solution.py:21
  31.7 9.7 %copy-start.3 = (f32[256,256]{1,0:T(8,128)S(1)}, f32[256,256]{1,0:T(8,128)}, u32[]{:S(2)}) copy-start(f32[256,256]{1,0:T(8,128)} %get-tuple-element.349) | copy-start | bytes 786436
  31.7 9.7 %copy-start.4 = (f32[256,256]{1,0:T(8,128)S(1)}, f32[256,256]{1,0:T(8,128)}, u32[]{:S(2)}) copy-start(f32[256,256]{1,0:T(8,128)} %get-tuple-element.350) | copy-start | bytes 786436
  91.5 3.2 copy-start
  94.7 186.2 %collective-permute-start.4 = (f32[2,1280,128]{2,1,0:T(8,128)}, f32[2,1280,128]{2,1,0:T(8,128)S(1)}, u32[]{:S(2)}, u32[]{:S(2)}) collective-permute-start(f32[2,1280,128]{2,1,0:T(8,128)} %get-tuple-element.341), channel_id=1, source_target_pairs={{0,1},{1,2},{2,3},{3,4},{4,5},{5,6},{6,7},{7,8},{8,9},{9,10},{10,1... | collective-permute-start | bytes 3932168 | tf_op jit(solution)/shard_map/ppermute | solution.py:20
  122.3 158.6 %collective-permute-start.5 = (f32[2,1280,128]{2,1,0:T(8,128)S(1)}, f32[2,1280,128]{2,1,0:T(8,128)}, u32[]{:S(2)}, u32[]{:S(2)}) collective-permute-start(f32[2,1280,128]{2,1,0:T(8,128)S(1)} %get-tuple-element.342), channel_id=1, source_target_pairs={{1,0},{2,1},{3,2},{4,3},{5,4},{6,5},{7,6},{8,7},{9,8},{10,9},{11,1... | collective-permute-start | bytes 3932168 | tf_op jit(solution)/shard_map/ppermute | solution.py:21
  282.8 24.8 %collective-permute-start.6 = (f32[2,128,128]{2,1,0:T(8,128)S(1)}, f32[2,128,128]{2,1,0:T(8,128)S(1)}, u32[]{:S(2)}, u32[]{:S(2)}) collective-permute-start(f32[2,128,128]{2,1,0:T(8,128)S(1)} %get-tuple-element.346), channel_id=1, source_target_pairs={{0,16},{1,17},{2,18},{3,19},{4,20},{5,21},{6,22},{7,23},{8,24},{9,... | collective-permute-start | bytes 393224 | tf_op jit(solution)/shard_map/ppermute | solution.py:20
  306.1 7.9 %copy-start.2 = (f32[2,1024,128]{2,1,0:T(8,128)S(1)}, f32[2,1024,128]{2,1,0:T(8,128)}, u32[]{:S(2)}) copy-start(f32[2,1024,128]{2,1,0:T(8,128)} %param.21) | copy-start | bytes 3145732
  306.2 7.8 %collective-permute-start.7 = (f32[2,128,128]{2,1,0:T(8,128)S(1)}, f32[2,128,128]{2,1,0:T(8,128)S(1)}, u32[]{:S(2)}, u32[]{:S(2)}) collective-permute-start(f32[2,128,128]{2,1,0:T(8,128)S(1)} %get-tuple-element.345), channel_id=1, source_target_pairs={{16,0},{17,1},{18,2},{19,3},{20,4},{21,5},{22,6},{23,7},{24,8},{25... | collective-permute-start | bytes 393224 | tf_op jit(solution)/shard_map/ppermute | solution.py:21
Sparse Core Ops, SparseCore 0:
  123.8 148.0 reduce-scatter.1
where the time goes:
time: 325 us; the launch traced here: 323 us
  waiting for transfers between devices  161 us (50%)
  starting transfers between devices  41.7 us (13%)
  blocking collectives  29.8 us (9%)
  matrix products  28.4 us (9%)
  local copies, waits for them, and re-layouts  27.6 us (8%)
  between operations  15 us (5%)
  other arithmetic  11.9 us (4%)
  loops' own time  7.08 us (2%)
    reduce_scatter x1, waiting for transfers between devices, on_device(): share = lax.psum_scatter(grad_probe, 'pos', scatter_dimension=1, tiled=True)  147 us
    ppermute x4, starting transfers between devices, padded(): before = lax.ppermute(last, axis, up)  36.3 us
    dot_general x16, matrix products, product(): jnp.dot(left, right, precision=lax.Precision.HIGHEST, preferred_element_t...  28.4 us
    all_gather x1, blocking collectives, on_device(): probe_new = lax.all_gather(new_rows, 'pos', axis=1, tiled=True)  20.9 us
    ppermute x4, waiting for transfers between devices, padded(): after = lax.ppermute(initial, axis, down)  12.9 us
    gather x9, local copies, waits for them, and re-layouts  9.58 us
    psum x1, blocking collectives, on_device(): share = lax.psum(share, 'grp')  8.97 us
  transfers between devices with their start and end apart: 9, of which 5 were waited for; matrix products, arithmetic and copies ran while one was open for 1% of the time, Pallas kernels for 0%

commit v1 on v0

--- a/solution.py
+++ b/solution.py
@@ -133,7 +133,12 @@
     row_share = M // pos_count
     mine = lax.dynamic_slice_in_dim(probe_field, pos_index * row_share, row_share, 1)
     new_rows = mine - step_probe * share / live_total
-    probe_new = lax.all_gather(new_rows, "pos", axis=1, tiled=True)
+    ring = [new_rows]
+    for hop in range(15):
+        ring.append(lax.ppermute(ring[-1], "pos", [(dev, (dev + 1) % 16) for dev in range(16)]))
+    probe_new = jnp.roll(
+        jnp.concatenate(ring[::-1], axis=1), (lax.axis_index("pos") + 1) * ring[0].shape[1], axis=1
+    )
     return (object_new, probe_new)
 
 

time: 325 us -> 402 us (1.24)
  the two profiles are of different devices: /device:TPU:0 before, /device:TPU:2 now
where the time goes in v1:
time: 402 us; the launch traced here: 400 us
  waiting for transfers between devices  276 us (69%)
  local copies, waits for them, and re-layouts  28.8 us (7%)
  matrix products  28.3 us (7%)
  starting transfers between devices  24.1 us (6%)
  between operations  15.2 us (4%)
  other arithmetic  11.8 us (3%)
  blocking collectives  8.91 us (2%)
  loops' own time  7.07 us (2%)
    reduce_scatter x1, waiting for transfers between devices, on_device(): share = lax.psum_scatter(grad_probe, 'pos', scatter_dimension=1, tiled=True)  144 us
    ppermute x15, waiting for transfers between devices, on_device(): lax.ppermute(ring[-1], 'pos', [(dev, (dev + 1) % 16) for dev in range(16)])  83.1 us
    ppermute x4, waiting for transfers between devices, padded(): before = lax.ppermute(last, axis, up)  41 us
    dot_general x16, matrix products, product(): jnp.dot(left, right, precision=lax.Precision.HIGHEST, preferred_element_t...  28.3 us
    ppermute x4, starting transfers between devices, padded(): after = lax.ppermute(initial, axis, down)  12.7 us
    gather x9, local copies, waits for them, and re-layouts  9.85 us
    ppermute x4, starting transfers between devices, padded(): before = lax.ppermute(last, axis, up)  9.73 us
    psum x1, blocking collectives, on_device(): share = lax.psum(share, 'grp')  8.91 us
  transfers between devices with their start and end apart: 24, of which 22 were waited for; matrix products, arithmetic and copies ran while one was open for 2% of the time, Pallas kernels for 0%

profile of v1, /device:TPU:2, one launch (start us, length us, event | category | flops | bytes accessed | tf_op | source)
XLA Modules:
  0.0 400.3 jit_solution(13909269058838925098)
XLA Ops:
  8.3 3.4 collective-permute-start
  15.8 2.8 collective-permute-done.1
  20.5 3.6 collective-permute-start.3
  25.8 25.8 %collective-permute-done.2 = f32[2,1280,128]{2,1,0:T(8,128)S(1)} collective-permute-done((f32[2,1280,128]{2,1,0:T(8,128)S(1)}, f32[2,1280,128]{2,1,0:T(8,128)S(1)}, u32[]{:S(2)}, u32[]{:S(2)}) %collective-permute-start.2) | collective-permute-done | bytes 1310752 | tf_op jit(solution)/shard_map/ppermute | solution.py:20
  51.6 3.4 pad_maximum_fusion
  55.2 9.9 %while.33 = (s32[]{:T(128)}, f32[2,1280,384]{2,1,0:T(8,128)}, s32[3,3]{1,0:T(4,128)S(1)}, f32[3,2,256,256]{3,2,1,0:T(8,128)S(1)}, s32[]{:T(128)}) while((s32[]{:T(128)}, f32[2,1280,384]{2,1,0:T(8,128)}, s32[3,3]{1,0:T(4,128)S(1)}, f32[3,2,256,256]{3,2,1,0:T(8,128)S(1)}, s32[]{:T(128)}) %tuple.101), condition=%wide.while_cond.4, body=%wide.while_body.4.sunk | while | flops 2 | bytes 1048693 | solution.py:76
  55.8 2.6 bitcast_dynamic-update-slice_fusion.2
  59.2 2.6 bitcast_dynamic-update-slice_fusion.2
  62.5 2.6 bitcast_dynamic-update-slice_fusion.2
  67.9 30.8 %while.34 = (s32[]{:T(128)}, f32[3,2,256,256]{3,2,1,0:T(8,128)}, s32[]{:T(128)}, f32[3,2,256,256]{3,2,1,0:T(8,128)}, f32[3,256,256]{2,1,0:T(8,128)}, /*index=5*/s32[]{:T(128)}, s32[]{:T(128)}, s32[]{:T(128)}, s32[]{}) while((s32[]{:T(128)}, f32[3,2,256,256]{3,2,1,0:T(8,128)}, s32[]{:T(128)}, ...), condition=%wide.region_1.2_spmd.clone.clone, body=%wide.region_0.1_spmd.clone.clone.sunk | while | flops 3238789120 | bytes 12320939 | solution.py:92
  100.9 15.7 %while.32 = (s32[]{:T(128)}, f32[2,1280,384]{2,1,0:T(8,128)}, f32[2,256,256]{2,1,0:T(8,128)S(1)}, s32[]{:T(128)}, s32[3]{0:T(128)S(1)}, /*index=5*/s32[3]{0:T(12...) while((s32[]{:T(128)}, f32[2,1280,384]{2,1,0:T(8,128)}, ...), condition=%wide.region_3.4_spmd, body=%wide.region_2.3_spmd.sunk | while | flops 1310731 | bytes 6816019 | solution.py:118
  109.3 6.5 %dynamic_update_slice.13 = f32[2,1280,384]{2,1,0:T(8,128)} dynamic-update-slice(f32[2,1280,384]{2,1,0:T(8,128)} %get-tuple-element.545, f32[2,256,256]{2,1,0:T(8,128)S(1)} %get-tuple-element.473, s32[]{:T(128)} %constant.196.clone.1..sunk, s32[]{:T(128)S(6)} %select_n.177, s32[]{:T(128)S(6)} %select_n.178) | dynamic-update-slice | bytes 1048580 | tf_op jit(solution)/shard_map/while/body/dynamic_update_slice | solution.py:111
  118.7 143.7 %reduce-scatter.2.cloned.1.call-done = f32[2,16,256]{2,1,0:T(8,128)} async-done(((f32[2,256,256]{2,1,0:T(8,128)}), f32[2,16,256]{2,1,0:T(8,128)}) %reduce-scatter.2.cloned.1.call-update) | async-done | bytes 32784 | tf_op jit(solution)/shard_map/reduce_scatter | solution.py:131
  262.4 8.9 %psum.7 = f32[2,16,256]{2,1,0:T(8,128)S(1)} all-reduce(f32[2,16,256]{2,1,0:T(8,128)} %reduce-scatter.2.cloned.1.call-done), channel_id=1, replica_groups=mesh['grp'=2,'pos'=16] {'grp'}, use_global_device_ids=true, to_apply=%region_5.6 | all-reduce | flops 8192 | bytes 65536 | tf_op jit(solution)/shard_map/psum | solution.py:132
  271.4 3.3 collective-permute-done.8
  274.7 3.3 collective-permute-done.9
  278.2 3.1 collective-permute-done.10
  282.5 4.0 collective-permute-done.11
  286.7 5.8 %collective-permute-done.12 = f32[2,16,256]{2,1,0:T(8,128)S(1)} collective-permute-done((f32[2,16,256]{2,1,0:T(8,128)S(1)}, f32[2,16,256]{2,1,0:T(8,128)S(1)}, u32[]{:S(2)}, u32[]{:S(2)}) %collective-permute-start.12) | collective-permute-done | bytes 32800 | tf_op jit(solution)/shard_map/ppermute | solution.py:138
  292.5 6.0 %collective-permute-done.13 = f32[2,16,256]{2,1,0:T(8,128)S(1)} collective-permute-done((f32[2,16,256]{2,1,0:T(8,128)S(1)}, f32[2,16,256]{2,1,0:T(8,128)S(1)}, u32[]{:S(2)}, u32[]{:S(2)}) %collective-permute-start.13) | collective-permute-done | bytes 32800 | tf_op jit(solution)/shard_map/ppermute | solution.py:138
  298.6 6.0 %collective-permute-done.14 = f32[2,16,256]{2,1,0:T(8,128)S(1)} collective-permute-done((f32[2,16,256]{2,1,0:T(8,128)S(1)}, f32[2,16,256]{2,1,0:T(8,128)S(1)}, u32[]{:S(2)}, u32[]{:S(2)}) %collective-permute-start.14) | collective-permute-done | bytes 32800 | tf_op jit(solution)/shard_map/ppermute | solution.py:138
  304.6 6.0 %collective-permute-done.15 = f32[2,16,256]{2,1,0:T(8,128)S(1)} collective-permute-done((f32[2,16,256]{2,1,0:T(8,128)S(1)}, f32[2,16,256]{2,1,0:T(8,128)S(1)}, u32[]{:S(2)}, u32[]{:S(2)}) %collective-permute-start.15) | collective-permute-done | bytes 32800 | tf_op jit(solution)/shard_map/ppermute | solution.py:138
  310.6 6.0 %collective-permute-done.16 = f32[2,16,256]{2,1,0:T(8,128)S(1)} collective-permute-done((f32[2,16,256]{2,1,0:T(8,128)S(1)}, f32[2,16,256]{2,1,0:T(8,128)S(1)}, u32[]{:S(2)}, u32[]{:S(2)}) %collective-permute-start.16) | collective-permute-done | bytes 32800 | tf_op jit(solution)/shard_map/ppermute | solution.py:138
  316.7 6.0 %collective-permute-done.17 = f32[2,16,256]{2,1,0:T(8,128)S(1)} collective-permute-done((f32[2,16,256]{2,1,0:T(8,128)S(1)}, f32[2,16,256]{2,1,0:T(8,128)S(1)}, u32[]{:S(2)}, u32[]{:S(2)}) %collective-permute-start.17) | collective-permute-done | bytes 32800 | tf_op jit(solution)/shard_map/ppermute | solution.py:138
  322.7 6.0 %collective-permute-done.18 = f32[2,16,256]{2,1,0:T(8,128)S(1)} collective-permute-done((f32[2,16,256]{2,1,0:T(8,128)S(1)}, f32[2,16,256]{2,1,0:T(8,128)S(1)}, u32[]{:S(2)}, u32[]{:S(2)}) %collective-permute-start.18) | collective-permute-done | bytes 32800 | tf_op jit(solution)/shard_map/ppermute | solution.py:138
  328.7 6.0 %collective-permute-done.19 = f32[2,16,256]{2,1,0:T(8,128)S(1)} collective-permute-done((f32[2,16,256]{2,1,0:T(8,128)S(1)}, f32[2,16,256]{2,1,0:T(8,128)S(1)}, u32[]{:S(2)}, u32[]{:S(2)}) %collective-permute-start.19) | collective-permute-done | bytes 32800 | tf_op jit(solution)/shard_map/ppermute | solution.py:138
  334.8 6.0 %collective-permute-done.20 = f32[2,16,256]{2,1,0:T(8,128)S(1)} collective-permute-done((f32[2,16,256]{2,1,0:T(8,128)S(1)}, f32[2,16,256]{2,1,0:T(8,128)S(1)}, u32[]{:S(2)}, u32[]{:S(2)}) %collective-permute-start.20) | collective-permute-done | bytes 32800 | tf_op jit(solution)/shard_map/ppermute | solution.py:138
  340.8 6.0 %collective-permute-done.21 = f32[2,16,256]{2,1,0:T(8,128)S(1)} collective-permute-done((f32[2,16,256]{2,1,0:T(8,128)S(1)}, f32[2,16,256]{2,1,0:T(8,128)S(1)}, u32[]{:S(2)}, u32[]{:S(2)}) %collective-permute-start.21) | collective-permute-done | bytes 32800 | tf_op jit(solution)/shard_map/ppermute | solution.py:138
  350.7 6.3 %collective-permute-start.5 = (f32[2,1280,128]{2,1,0:T(8,128)S(1)}, f32[2,1280,128]{2,1,0:T(8,128)S(1)}, u32[]{:S(2)}, u32[]{:S(2)}) collective-permute-start(f32[2,1280,128]{2,1,0:T(8,128)S(1)} %get-tuple-element.342), channel_id=1, source_target_pairs={{1,0},{2,1},{3,2},{4,3},{5,4},{6,5},{7,6},{8,7},{9,8},{10,9},{11,1... | collective-permute-start | bytes 3932168 | tf_op jit(solution)/shard_map/ppermute | solution.py:21
  357.0 9.2 %collective-permute-done.22 = f32[2,16,256]{2,1,0:T(8,128)S(1)} collective-permute-done((f32[2,16,256]{2,1,0:T(8,128)S(1)}, f32[2,16,256]{2,1,0:T(8,128)S(1)}, u32[]{:S(2)}, u32[]{:S(2)}) %collective-permute-start.22) | collective-permute-done | bytes 32800 | tf_op jit(solution)/shard_map/ppermute | solution.py:138
  366.6 13.7 %collective-permute-done.4 = f32[2,1280,128]{2,1,0:T(8,128)S(1)} collective-permute-done((f32[2,1280,128]{2,1,0:T(8,128)S(1)}, f32[2,1280,128]{2,1,0:T(8,128)S(1)}, u32[]{:S(2)}, u32[]{:S(2)}) %collective-permute-start.4) | collective-permute-done | bytes 1310752 | tf_op jit(solution)/shard_map/ppermute | solution.py:20
  386.9 5.4 %collective-permute-done.7 = f32[2,128,128]{2,1,0:T(8,128)S(1)} collective-permute-done((f32[2,128,128]{2,1,0:T(8,128)S(1)}, f32[2,128,128]{2,1,0:T(8,128)S(1)}, u32[]{:S(2)}, u32[]{:S(2)}) %collective-permute-start.7) | collective-permute-done | bytes 131104 | tf_op jit(solution)/shard_map/ppermute | solution.py:21
  (124 shorter events, 63.4 us)
Async XLA Ops:
  7.2 17.0 %copy-start.4 = (s32[2,3]{1,0:T(2,128)S(1)}, s32[2,3]{1,0:T(2,128)}, u32[]{:S(2)}) copy-start(s32[2,3]{1,0:T(2,128)} %param.24) | copy-start | bytes 76
  7.2 17.2 %copy-start.5 = (s32[32]{0:T(128)S(1)}, s32[32]{0:T(128)}, u32[]{:S(2)}) copy-start(s32[32]{0:T(128)} %param.25) | copy-start | bytes 388
  7.2 17.8 %copy-start.1 = (f32[2,256,256]{2,1,0:T(8,128)S(1)}, f32[2,256,256]{2,1,0:T(8,128)}, u32[]{:S(2)}) copy-start(f32[2,256,256]{2,1,0:T(8,128)} %param.22) | copy-start | bytes 1572868
  7.2 255.2 %reduce-scatter.2.cloned.1.call-start = ((), (), s32[]{:S(2)}) async-start(), calls=%async_computation.1 | async-start | bytes 557056 | tf_op jit(solution)/shard_map/reduce_scatter | solution.py:131
  8.3 6.2 %collective-permute-start = (f32[2,128,128]{2,1,0:T(8,128)S(1)}, f32[2,128,128]{2,1,0:T(8,128)S(1)}, u32[]{:S(2)}, u32[]{:S(2)}) collective-permute-start(f32[2,128,128]{2,1,0:T(8,128)S(1)} %get-tuple-element.348), channel_id=1, source_target_pairs={{0,16},{1,17},{2,18},{3,19},{4,20},{5,21},{6,22},{7,23},{8,24},{9,... | collective-permute-start | bytes 393224 | tf_op jit(solution)/shard_map/ppermute | solution.py:20
  11.7 6.9 %collective-permute-start.1 = (f32[2,128,128]{2,1,0:T(8,128)S(1)}, f32[2,128,128]{2,1,0:T(8,128)S(1)}, u32[]{:S(2)}, u32[]{:S(2)}) collective-permute-start(f32[2,128,128]{2,1,0:T(8,128)S(1)} %get-tuple-element.347), channel_id=1, source_target_pairs={{16,0},{17,1},{18,2},{19,3},{20,4},{21,5},{22,6},{23,7},{24,8},{25... | collective-permute-start | bytes 393224 | tf_op jit(solution)/shard_map/ppermute | solution.py:21
  18.6 33.0 %collective-permute-start.2 = (f32[2,1280,128]{2,1,0:T(8,128)S(1)}, f32[2,1280,128]{2,1,0:T(8,128)S(1)}, u32[]{:S(2)}, u32[]{:S(2)}) collective-permute-start(f32[2,1280,128]{2,1,0:T(8,128)S(1)} %constant_dynamic-update-slice_fusion), channel_id=1, source_target_pairs={{0,1},{1,2},{2,3},{3,4},{4,5},{5,6},{6,7},{7,8},{8,9},{9,10},{10,1... | collective-permute-start | bytes 3932168 | tf_op jit(solution)/shard_map/ppermute | solution.py:20
  20.5 31.0 %collective-permute-start.3 = (f32[2,1280,128]{2,1,0:T(8,128)S(1)}, f32[2,1280,128]{2,1,0:T(8,128)}, u32[]{:S(2)}, u32[]{:S(2)}) collective-permute-start(f32[2,1280,128]{2,1,0:T(8,128)S(1)} %constant_dynamic-update-slice_fusion), channel_id=1, source_target_pairs={{1,0},{2,1},{3,2},{4,3},{5,4},{6,5},{7,6},{8,7},{9,8},{10,9},{11,1... | collective-permute-start | bytes 3932168 | tf_op jit(solution)/shard_map/ppermute | solution.py:21
  55.1 9.9 %copy-start.3 = (f32[256,256]{1,0:T(8,128)S(1)}, f32[256,256]{1,0:T(8,128)}, u32[]{:S(2)}) copy-start(f32[256,256]{1,0:T(8,128)} %get-tuple-element.350) | copy-start | bytes 786436
  116.6 0.8 copy-start
  271.3 3.4 collective-permute-start.8
  274.7 3.3 collective-permute-start.9
  278.0 3.3 collective-permute-start.10
  281.4 5.1 %collective-permute-start.11 = (f32[2,16,256]{2,1,0:T(8,128)S(1)}, f32[2,16,256]{2,1,0:T(8,128)S(1)}, u32[]{:S(2)}, u32[]{:S(2)}) collective-permute-start(f32[2,16,256]{2,1,0:T(8,128)S(1)} %collective-permute-done.10), channel_id=1, source_target_pairs={{0,1},{1,2},{2,3},{3,4},{4,5},{5,6},{6,7},{7,8},{8,9},{9,10},{10,1... | collective-permute-start | bytes 98312 | tf_op jit(solution)/shard_map/ppermute | solution.py:138
  286.5 6.0 %collective-permute-start.12 = (f32[2,16,256]{2,1,0:T(8,128)S(1)}, f32[2,16,256]{2,1,0:T(8,128)S(1)}, u32[]{:S(2)}, u32[]{:S(2)}) collective-permute-start(f32[2,16,256]{2,1,0:T(8,128)S(1)} %collective-permute-done.11), channel_id=1, source_target_pairs={{0,1},{1,2},{2,3},{3,4},{4,5},{5,6},{6,7},{7,8},{8,9},{9,10},{10,1... | collective-permute-start | bytes 98312 | tf_op jit(solution)/shard_map/ppermute | solution.py:138
  292.5 6.0 %collective-permute-start.13 = (f32[2,16,256]{2,1,0:T(8,128)S(1)}, f32[2,16,256]{2,1,0:T(8,128)S(1)}, u32[]{:S(2)}, u32[]{:S(2)}) collective-permute-start(f32[2,16,256]{2,1,0:T(8,128)S(1)} %collective-permute-done.12), channel_id=1, source_target_pairs={{0,1},{1,2},{2,3},{3,4},{4,5},{5,6},{6,7},{7,8},{8,9},{9,10},{10,1... | collective-permute-start | bytes 98312 | tf_op jit(solution)/shard_map/ppermute | solution.py:138
  298.6 6.0 %collective-permute-start.14 = (f32[2,16,256]{2,1,0:T(8,128)S(1)}, f32[2,16,256]{2,1,0:T(8,128)S(1)}, u32[]{:S(2)}, u32[]{:S(2)}) collective-permute-start(f32[2,16,256]{2,1,0:T(8,128)S(1)} %collective-permute-done.13), channel_id=1, source_target_pairs={{0,1},{1,2},{2,3},{3,4},{4,5},{5,6},{6,7},{7,8},{8,9},{9,10},{10,1... | collective-permute-start | bytes 98312 | tf_op jit(solution)/shard_map/ppermute | solution.py:138
  304.6 6.0 %collective-permute-start.15 = (f32[2,16,256]{2,1,0:T(8,128)S(1)}, f32[2,16,256]{2,1,0:T(8,128)S(1)}, u32[]{:S(2)}, u32[]{:S(2)}) collective-permute-start(f32[2,16,256]{2,1,0:T(8,128)S(1)} %collective-permute-done.14), channel_id=1, source_target_pairs={{0,1},{1,2},{2,3},{3,4},{4,5},{5,6},{6,7},{7,8},{8,9},{9,10},{10,1... | collective-permute-start | bytes 98312 | tf_op jit(solution)/shard_map/ppermute | solution.py:138
  310.6 6.0 %collective-permute-start.16 = (f32[2,16,256]{2,1,0:T(8,128)S(1)}, f32[2,16,256]{2,1,0:T(8,128)S(1)}, u32[]{:S(2)}, u32[]{:S(2)}) collective-permute-start(f32[2,16,256]{2,1,0:T(8,128)S(1)} %collective-permute-done.15), channel_id=1, source_target_pairs={{0,1},{1,2},{2,3},{3,4},{4,5},{5,6},{6,7},{7,8},{8,9},{9,10},{10,1... | collective-permute-start | bytes 98312 | tf_op jit(solution)/shard_map/ppermute | solution.py:138
  316.7 6.0 %collective-permute-start.17 = (f32[2,16,256]{2,1,0:T(8,128)S(1)}, f32[2,16,256]{2,1,0:T(8,128)S(1)}, u32[]{:S(2)}, u32[]{:S(2)}) collective-permute-start(f32[2,16,256]{2,1,0:T(8,128)S(1)} %collective-permute-done.16), channel_id=1, source_target_pairs={{0,1},{1,2},{2,3},{3,4},{4,5},{5,6},{6,7},{7,8},{8,9},{9,10},{10,1... | collective-permute-start | bytes 98312 | tf_op jit(solution)/shard_map/ppermute | solution.py:138
  322.7 6.0 %collective-permute-start.18 = (f32[2,16,256]{2,1,0:T(8,128)S(1)}, f32[2,16,256]{2,1,0:T(8,128)S(1)}, u32[]{:S(2)}, u32[]{:S(2)}) collective-permute-start(f32[2,16,256]{2,1,0:T(8,128)S(1)} %collective-permute-done.17), channel_id=1, source_target_pairs={{0,1},{1,2},{2,3},{3,4},{4,5},{5,6},{6,7},{7,8},{8,9},{9,10},{10,1... | collective-permute-start | bytes 98312 | tf_op jit(solution)/shard_map/ppermute | solution.py:138
  328.7 6.0 %collective-permute-start.19 = (f32[2,16,256]{2,1,0:T(8,128)S(1)}, f32[2,16,256]{2,1,0:T(8,128)S(1)}, u32[]{:S(2)}, u32[]{:S(2)}) collective-permute-start(f32[2,16,256]{2,1,0:T(8,128)S(1)} %collective-permute-done.18), channel_id=1, source_target_pairs={{0,1},{1,2},{2,3},{3,4},{4,5},{5,6},{6,7},{7,8},{8,9},{9,10},{10,1... | collective-permute-start | bytes 98312 | tf_op jit(solution)/shard_map/ppermute | solution.py:138
  334.8 6.0 %collective-permute-start.20 = (f32[2,16,256]{2,1,0:T(8,128)S(1)}, f32[2,16,256]{2,1,0:T(8,128)S(1)}, u32[]{:S(2)}, u32[]{:S(2)}) collective-permute-start(f32[2,16,256]{2,1,0:T(8,128)S(1)} %collective-permute-done.19), channel_id=1, source_target_pairs={{0,1},{1,2},{2,3},{3,4},{4,5},{5,6},{6,7},{7,8},{8,9},{9,10},{10,1... | collective-permute-start | bytes 98312 | tf_op jit(solution)/shard_map/ppermute | solution.py:138
  340.8 6.0 %collective-permute-start.21 = (f32[2,16,256]{2,1,0:T(8,128)S(1)}, f32[2,16,256]{2,1,0:T(8,128)S(1)}, u32[]{:S(2)}, u32[]{:S(2)}) collective-permute-start(f32[2,16,256]{2,1,0:T(8,128)S(1)} %collective-permute-done.20), channel_id=1, source_target_pairs={{0,1},{1,2},{2,3},{3,4},{4,5},{5,6},{6,7},{7,8},{8,9},{9,10},{10,1... | collective-permute-start | bytes 98312 | tf_op jit(solution)/shard_map/ppermute | solution.py:138
  346.9 19.4 %collective-permute-start.22 = (f32[2,16,256]{2,1,0:T(8,128)S(1)}, f32[2,16,256]{2,1,0:T(8,128)S(1)}, u32[]{:S(2)}, u32[]{:S(2)}) collective-permute-start(f32[2,16,256]{2,1,0:T(8,128)S(1)} %collective-permute-done.21), channel_id=1, source_target_pairs={{0,1},{1,2},{2,3},{3,4},{4,5},{5,6},{6,7},{7,8},{8,9},{9,10},{10,1... | collective-permute-start | bytes 98312 | tf_op jit(solution)/shard_map/ppermute | solution.py:138
  348.8 31.5 %collective-permute-start.4 = (f32[2,1280,128]{2,1,0:T(8,128)S(1)}, f32[2,1280,128]{2,1,0:T(8,128)S(1)}, u32[]{:S(2)}, u32[]{:S(2)}) collective-permute-start(f32[2,1280,128]{2,1,0:T(8,128)S(1)} %get-tuple-element.341), channel_id=1, source_target_pairs={{0,1},{1,2},{2,3},{3,4},{4,5},{5,6},{6,7},{7,8},{8,9},{9,10},{10,1... | collective-permute-start | bytes 3932168 | tf_op jit(solution)/shard_map/ppermute | solution.py:20
  350.7 29.6 %collective-permute-start.5 = (f32[2,1280,128]{2,1,0:T(8,128)S(1)}, f32[2,1280,128]{2,1,0:T(8,128)S(1)}, u32[]{:S(2)}, u32[]{:S(2)}) collective-permute-start(f32[2,1280,128]{2,1,0:T(8,128)S(1)} %get-tuple-element.342), channel_id=1, source_target_pairs={{1,0},{2,1},{3,2},{4,3},{5,4},{6,5},{7,6},{8,7},{9,8},{10,9},{11,1... | collective-permute-start | bytes 3932168 | tf_op jit(solution)/shard_map/ppermute | solution.py:21
  381.9 5.0 %collective-permute-start.6 = (f32[2,128,128]{2,1,0:T(8,128)S(1)}, f32[2,128,128]{2,1,0:T(8,128)S(1)}, u32[]{:S(2)}, u32[]{:S(2)}) collective-permute-start(f32[2,128,128]{2,1,0:T(8,128)S(1)} %get-tuple-element.346), channel_id=1, source_target_pairs={{0,16},{1,17},{2,18},{3,19},{4,20},{5,21},{6,22},{7,23},{8,24},{9,... | collective-permute-start | bytes 393224 | tf_op jit(solution)/shard_map/ppermute | solution.py:20
  385.2 7.1 %copy-start.2 = (f32[2,1024,128]{2,1,0:T(8,128)S(1)}, f32[2,1024,128]{2,1,0:T(8,128)}, u32[]{:S(2)}) copy-start(f32[2,1024,128]{2,1,0:T(8,128)} %param.21) | copy-start | bytes 3145732
  385.3 7.0 %collective-permute-start.7 = (f32[2,128,128]{2,1,0:T(8,128)S(1)}, f32[2,128,128]{2,1,0:T(8,128)S(1)}, u32[]{:S(2)}, u32[]{:S(2)}) collective-permute-start(f32[2,128,128]{2,1,0:T(8,128)S(1)} %get-tuple-element.345), channel_id=1, source_target_pairs={{16,0},{17,1},{18,2},{19,3},{20,4},{21,5},{22,6},{23,7},{24,8},{25... | collective-permute-start | bytes 393224 | tf_op jit(solution)/shard_map/ppermute | solution.py:21
Sparse Core Ops, SparseCore 0:
  117.5 144.8 reduce-scatter.1
